TPU v7x, 1024 devices: a whole 8x8x8 slice. The times are simulated.
1024 devices in a mesh: dp: 64 (over y, x), ctx: 16 (over z, core).
Axes of the slice: x: 8, y: 8, z: 8, core: 2. Of those that a mesh axis runs over, the one named last changes fastest.
Arguments:
- queries: bfloat16 [131072, 512], P(('dp', 'ctx')), may hold values from -25 to 25
- keys: bfloat16 [131072, 128], P(('dp', 'ctx')), may hold values from -6 to 6
- values: bfloat16 [131072, 128], P(('dp', 'ctx')), may hold values from -6 to 6
- out_grad: bfloat16 [131072, 512], P(('dp', 'ctx')), may hold values from -7 to 7
- doc_lengths: int32 [64, 65], P('dp'), may hold values from 0 to 2048, as said below
- source_slot: int32 [131072], P(('dp', 'ctx')), may hold values from 0 to 127, as said below
Outputs:
- attended: bfloat16 [131072, 512], P(('dp', 'ctx'))
- query_grad: bfloat16 [131072, 512], P(('dp', 'ctx'))
- key_grad: bfloat16 [131072, 128], P(('dp', 'ctx'))
- value_grad: bfloat16 [131072, 128], P(('dp', 'ctx'))
Inputs may be any that keep to these rules, and one draw needn't show every extreme that they name: `doc_lengths`: row d lists group d's documents in order: the first covers devices 0 to m - 1 of the group whole (m * 128 tokens, 1 <= m <= 16, with m = 16 in row 0), then 4 documents of positive length for each later device that fill that device exactly, then zeros; every row sums to 2048. `source_slot`: on each device the 128 entries are a permutation of 0 to 127.
All inputs are finite; a program needn't handle non-finite values.
Results may differ from a plain program's by a relative error of at most 0.033.
Values may be sent and summed in bfloat16 or wider, within the bound.
A program may use at most 32 MiB of HBM per device.

v0:
```python
import math

import jax
import jax.numpy as jnp
from jax import lax
from jax.sharding import PartitionSpec as P


def contract(left, right):
    return lax.dot_general(
        left, right, (((1,), (1,)), ((), ())), preferred_element_type=jnp.float32
    )


def contract_rows(left, right):
    return lax.dot_general(
        left, right, (((0,), (0,)), ((), ())), preferred_element_type=jnp.float32
    )


def spread(vector, copies):
    return jnp.broadcast_to(vector[:, None], (vector.shape[0], copies)).reshape(-1)


def visible(query_doc, query_pos, key_doc, key_pos):
    return (query_doc[:, None] == key_doc[None, :]) & (key_pos[None, :] <= query_pos[:, None])


def local(queries, keys, values, out_grad, doc_lengths, source_slot):
    row_count = queries.shape[0]
    head_width = keys.shape[1]
    head_count = queries.shape[1] // head_width
    score_scale = head_width ** (-0.5)
    arrived = (
        lax.all_to_all(queries, "dp", split_axis=0, concat_axis=0, tiled=True),
        lax.all_to_all(keys, "dp", split_axis=0, concat_axis=0, tiled=True),
        lax.all_to_all(values, "dp", split_axis=0, concat_axis=0, tiled=True),
        lax.all_to_all(out_grad, "dp", split_axis=0, concat_axis=0, tiled=True),
    )
    query_local = jnp.take(arrived[0], source_slot, axis=0)
    key_local = jnp.take(arrived[1], source_slot, axis=0)
    value_local = jnp.take(arrived[2], source_slot, axis=0)
    grad_local = jnp.take(arrived[3], source_slot, axis=0)
    key_all, value_all = (
        lax.all_gather(key_local, "ctx", axis=0, tiled=True),
        lax.all_gather(value_local, "ctx", axis=0, tiled=True),
    )
    group_rows = key_all.shape[0]
    first_row = lax.axis_index("ctx") * row_count
    key_pos = jnp.arange(group_rows, dtype=jnp.int32)
    doc_ends = jnp.cumsum(doc_lengths[0], dtype=jnp.int32)
    key_doc = jnp.sum(
        (key_pos[:, None] >= doc_ends[None, :]).astype(jnp.int32), axis=1, dtype=jnp.int32
    )
    own_pos = first_row + jnp.arange(row_count, dtype=jnp.int32)
    own_doc = lax.dynamic_slice_in_dim(key_doc, first_row, row_count)
    query_pos = spread(own_pos, head_count)
    query_doc = spread(own_doc, head_count)
    query_flat = query_local.reshape(row_count * head_count, head_width)
    grad_flat = grad_local.reshape(row_count * head_count, head_width)
    query_count = row_count * head_count
    block_rows = math.gcd(group_rows, 512)
    block_count = group_rows // block_rows

    def key_block(start, size):
        key_part = lax.dynamic_slice_in_dim(key_all, start, size)
        value_part = lax.dynamic_slice_in_dim(value_all, start, size)
        seen_mask = visible(
            query_doc,
            query_pos,
            lax.dynamic_slice_in_dim(key_doc, start, size),
            lax.dynamic_slice_in_dim(key_pos, start, size),
        )
        return (key_part, value_part, seen_mask)

    def max_step(step_index, carry_in):
        key_part, value_part, seen_mask = key_block(step_index * block_rows, block_rows)
        running_max, running_sum = carry_in
        score = jnp.where(seen_mask, contract(query_flat, key_part) * score_scale, -1e30)
        new_max = jnp.maximum(running_max, jnp.max(score, axis=1))
        weights = jnp.where(seen_mask, jnp.exp(score - new_max[:, None]), 0.0)
        return (new_max, running_sum * jnp.exp(running_max - new_max) + jnp.sum(weights, axis=1))

    start_state = (
        jnp.full((query_count,), -1e30, jnp.float32),
        jnp.zeros((query_count,), jnp.float32),
    )
    running_max, running_sum = lax.fori_loop(0, block_count, max_step, start_state)
    log_total = running_max + jnp.log(running_sum)

    def probs_of(query_part, key_part, seen_mask, totals):
        score = contract(query_part, key_part) * score_scale
        return jnp.where(seen_mask, jnp.exp(score - totals[:, None]), 0.0)

    def out_step(step_index, carry_in):
        key_part, value_part, seen_mask = key_block(step_index * block_rows, block_rows)
        probs_low = probs_of(query_flat, key_part, seen_mask, log_total).astype(jnp.bfloat16)
        return carry_in + jnp.dot(probs_low, value_part, preferred_element_type=jnp.float32)

    attended_sum = lax.fori_loop(
        0, block_count, out_step, jnp.zeros((query_count, head_width), jnp.float32)
    )
    attended_low = attended_sum.astype(jnp.bfloat16)
    row_delta = jnp.sum(grad_flat.astype(jnp.float32) * attended_low.astype(jnp.float32), axis=1)

    def query_step(step_index, carry_in):
        key_part, value_part, seen_mask = key_block(step_index * block_rows, block_rows)
        probs = probs_of(query_flat, key_part, seen_mask, log_total)
        prob_grad = contract(grad_flat, value_part)
        score_grad = (probs * (prob_grad - row_delta[:, None])).astype(jnp.bfloat16)
        return carry_in + jnp.dot(score_grad, key_part, preferred_element_type=jnp.float32)

    query_sum = lax.fori_loop(
        0, block_count, query_step, jnp.zeros((query_count, head_width), jnp.float32)
    )
    query_grad_low = (query_sum * score_scale).astype(jnp.bfloat16)
    own_stats = jnp.concatenate(
        [log_total.reshape(row_count, head_count), row_delta.reshape(row_count, head_count)], axis=1
    )
    group_stats = lax.all_gather(own_stats, "ctx", axis=0, tiled=True)
    query_piece = lax.all_gather(query_local, "ctx", axis=0, tiled=True)
    grad_piece = lax.all_gather(grad_local, "ctx", axis=0, tiled=True)
    size = query_piece.shape[0]
    piece_rows = math.gcd(size, 128)

    def piece_step(piece_index, carry_part):
        offset = piece_index * piece_rows
        query_part = lax.dynamic_slice_in_dim(query_piece, offset, piece_rows).reshape(
            piece_rows * head_count, head_width
        )
        grad_part = lax.dynamic_slice_in_dim(grad_piece, offset, piece_rows).reshape(
            piece_rows * head_count, head_width
        )
        stat_rows = lax.dynamic_slice_in_dim(group_stats, offset, piece_rows)
        piece_total = stat_rows[:, :head_count].reshape(-1)
        piece_delta = stat_rows[:, head_count:].reshape(-1)
        positions = offset + jnp.arange(piece_rows, dtype=jnp.int32)
        piece_doc = lax.dynamic_slice_in_dim(key_doc, offset, piece_rows)
        seen_mask = visible(
            spread(piece_doc, head_count), spread(positions, head_count), own_doc, own_pos
        )
        probs = probs_of(query_part, key_local, seen_mask, piece_total)
        value_term = contract_rows(probs.astype(jnp.bfloat16), grad_part)
        prob_grad = contract(grad_part, value_local)
        score_grad = (probs * (prob_grad - piece_delta[:, None])).astype(jnp.bfloat16)
        key_term = contract_rows(score_grad, query_part) * score_scale
        return carry_part + jnp.concatenate([key_term, value_term], axis=1)

    key_value_sum = lax.fori_loop(
        0, size // piece_rows, piece_step, jnp.zeros((row_count, 2 * head_width), jnp.float32)
    )
    key_grad_low = key_value_sum[:, :head_width].astype(jnp.bfloat16)
    value_grad_low = key_value_sum[:, head_width:].astype(jnp.bfloat16)

    def placed(computed):
        return jnp.zeros_like(computed).at[source_slot].set(computed)

    returned = (
        lax.all_to_all(
            placed(attended_low.reshape(row_count, head_count * head_width)),
            "dp",
            split_axis=0,
            concat_axis=0,
            tiled=True,
        ),
        lax.all_to_all(
            placed(query_grad_low.reshape(row_count, head_count * head_width)),
            "dp",
            split_axis=0,
            concat_axis=0,
            tiled=True,
        ),
        lax.all_to_all(placed(key_grad_low), "dp", split_axis=0, concat_axis=0, tiled=True),
        lax.all_to_all(placed(value_grad_low), "dp", split_axis=0, concat_axis=0, tiled=True),
    )
    return (returned[0], returned[1], returned[2], returned[3])


def solution(mesh):
    placed = (
        P(("dp", "ctx"), None),
        P(("dp", "ctx"), None),
        P(("dp", "ctx"), None),
        P(("dp", "ctx"), None),
        P("dp", None),
        P(("dp", "ctx")),
    )
    return jax.shard_map(
        local,
        mesh=mesh,
        in_specs=placed,
        out_specs=(
            P(("dp", "ctx"), None),
            P(("dp", "ctx"), None),
            P(("dp", "ctx"), None),
            P(("dp", "ctx"), None),
        ),
        check_vma=False,
    )
```

profile of v0, /device:TPU:1, one launch (start us, length us, event | category | flops | bytes accessed | tf_op | source)
XLA Modules:
  0.0 289.6 jit_solution(1641095962417840871)
XLA Ops:
  7.2 1.6 all_to_all.67
  8.8 14.0 %all-to-all-start.1 = ((bf16[64,2,512]{2,1,0:T(2,128)(2,1)}), bf16[64,2,512]{2,1,0:T(2,128)(2,1)S(1)}, u32[]{:S(2)}, u32[]{:S(2)}) async-start(bf16[64,2,512]{2,1,0:T(2,128)(2,1)} %all_to_all.67), calls=%async_computation.1 | async-start | bytes 262144 | tf_op jit(solution)/shard_map/all_to_all | solution.py:35
  22.8 1.6 all_to_all.76
  25.1 9.3 %all-to-all-done.1 = bf16[64,2,512]{2,1,0:T(2,128)(2,1)S(1)} async-done(((bf16[64,2,512]{2,1,0:T(2,128)(2,1)}), bf16[64,2,512]{2,1,0:T(2,128)(2,1)S(1)}, u32[]{:S(2)}, u32[]{:S(2)}) %all-to-all-start.1) | async-done | bytes 131104 | tf_op jit(solution)/shard_map/all_to_all | solution.py:35
  34.4 4.6 %all-to-all-start.4 = ((bf16[64,2,512]{2,1,0:T(2,128)(2,1)}), bf16[64,2,512]{2,1,0:T(2,128)(2,1)S(1)}, u32[]{:S(2)}, u32[]{:S(2)}) async-start(bf16[64,2,512]{2,1,0:T(2,128)(2,1)} %all_to_all.76), calls=%async_computation.4 | async-start | bytes 262144 | tf_op jit(solution)/shard_map/all_to_all | solution.py:38
  40.6 9.9 %all-to-all-done.4 = bf16[64,2,512]{2,1,0:T(2,128)(2,1)S(1)} async-done(((bf16[64,2,512]{2,1,0:T(2,128)(2,1)}), bf16[64,2,512]{2,1,0:T(2,128)(2,1)S(1)}, u32[]{:S(2)}, u32[]{:S(2)}) %all-to-all-start.4) | async-done | bytes 131104 | tf_op jit(solution)/shard_map/all_to_all | solution.py:38
  52.3 4.7 %all-to-all-start.2 = ((bf16[64,2,128]{2,1,0:T(2,128)(2,1)}), bf16[64,2,128]{2,1,0:T(2,128)(2,1)S(1)}, u32[]{:S(2)}, u32[]{:S(2)}) async-start(bf16[64,2,128]{2,1,0:T(2,128)(2,1)} %bitcast.3), calls=%async_computation.2 | async-start | bytes 65536 | tf_op jit(solution)/shard_map/all_to_all | solution.py:37
  57.7 10.2 %all-to-all-done.2 = bf16[64,2,128]{2,1,0:T(2,128)(2,1)S(1)} async-done(((bf16[64,2,128]{2,1,0:T(2,128)(2,1)}), bf16[64,2,128]{2,1,0:T(2,128)(2,1)S(1)}, u32[]{:S(2)}, u32[]{:S(2)}) %all-to-all-start.2) | async-done | bytes 32800 | tf_op jit(solution)/shard_map/all_to_all | solution.py:37
  67.8 4.6 %all-to-all-start = ((bf16[64,2,128]{2,1,0:T(2,128)(2,1)}), bf16[64,2,128]{2,1,0:T(2,128)(2,1)S(1)}, u32[]{:S(2)}, u32[]{:S(2)}) async-start(bf16[64,2,128]{2,1,0:T(2,128)(2,1)} %bitcast.1), calls=%async_computation | async-start | bytes 65536 | tf_op jit(solution)/shard_map/all_to_all | solution.py:36
  73.2 10.0 %all-to-all-done = bf16[64,2,128]{2,1,0:T(2,128)(2,1)S(1)} async-done(((bf16[64,2,128]{2,1,0:T(2,128)(2,1)}), bf16[64,2,128]{2,1,0:T(2,128)(2,1)S(1)}, u32[]{:S(2)}, u32[]{:S(2)}) %all-to-all-start) | async-done | bytes 32800 | tf_op jit(solution)/shard_map/all_to_all | solution.py:36
  84.0 36.4 %all_gather.15 = bf16[2048,128]{1,0:T(8,128)(2,1)S(1)} all-gather(bf16[128,128]{1,0:T(8,128)(2,1)S(1)} %get-tuple-element.1371), channel_id=1, replica_groups=mesh['dp'=64,'ctx'=16] {'ctx'}, dimensions={0}, use_global_device_ids=true | all-gather | bytes 557056 | tf_op jit(solution)/shard_map/all_gather | solution.py:45
  120.4 15.9 %all_gather.16 = bf16[2048,128]{1,0:T(8,128)(2,1)S(1)} all-gather(bf16[128,128]{1,0:T(8,128)(2,1)S(1)} %get-tuple-element.1374), channel_id=1, replica_groups=mesh['dp'=64,'ctx'=16] {'ctx'}, dimensions={0}, use_global_device_ids=true | all-gather | bytes 557056 | tf_op jit(solution)/shard_map/all_gather | solution.py:46
  136.4 5.3 %while.58 = (s32[]{:T(128)}, f32[512]{0:T(512)S(1)}, f32[512]{0:T(512)S(1)}, s32[2048]{0:T(1024)S(1)}, s32[2048]{0:T(1024)S(1)}, /*index=5*/bf16[2048,128]{1,0:T...) while((s32[]{:T(128)}, f32[512]{0:T(512)S(1)}, ...), condition=%wide.region_5.8_spmd.clone, body=%wide.region_2.7_spmd.clone.sunk | while | flops 70257160 | bytes 2424010 | solution.py:88
  141.9 5.4 %while.59 = (s32[]{:T(128)}, f32[512,128]{1,0:T(8,128)S(1)}, s32[2048]{0:T(1024)S(1)}, s32[2048]{0:T(1024)S(1)}, bf16[2048,128]{1,0:T(8,128)(2,1)S(1)}, /*index=...) while((s32[]{:T(128)}, f32[512,128]{1,0:T(8,128)S(1)}, ...), condition=%wide.region_7.10_spmd.clone, body=%wide.region_6.9_spmd.clone.sunk | while | flops 136183808 | bytes 950988 | solution.py:100
  149.3 4.8 %all-to-all-start.3 = ((bf16[64,2,512]{2,1,0:T(2,128)(2,1)}), bf16[64,2,512]{2,1,0:T(2,128)(2,1)S(1)}, u32[]{:S(2)}, u32[]{:S(2)}) async-start(bf16[64,2,512]{2,1,0:T(2,128)(2,1)} %all_to_all.73), calls=%async_computation.3 | async-start | bytes 262144 | tf_op jit(solution)/shard_map/all_to_all | solution.py:159
  154.1 6.7 %while.60 = (s32[]{:T(128)}, f32[512,128]{1,0:T(8,128)S(1)}, s32[2048]{0:T(1024)S(1)}, s32[2048]{0:T(1024)S(1)}, bf16[2048,128]{1,0:T(8,128)(2,1)S(1)}, /*index=...) while((s32[]{:T(128)}, f32[512,128]{1,0:T(8,128)S(1)}, ...), condition=%wide.region_11.14_spmd.clone, body=%wide.region_10.13_spmd.clone.sunk | while | flops 203816960 | bytes 3312352 | solution.py:113
  163.1 16.0 %all_gather.18 = f32[2048,8]{0,1:T(8,128)S(1)} all-gather(f32[128,8]{0,1:T(8,128)S(1)} %pad_maximum_fusion), channel_id=1, replica_groups=mesh['dp'=64,'ctx'=16] {'ctx'}, dimensions={0}, use_global_device_ids=true | all-gather | bytes 69632 | tf_op jit(solution)/shard_map/all_gather | solution.py:120
  179.1 12.2 %all-to-all-start.5 = ((bf16[64,2,512]{2,1,0:T(2,128)(2,1)}), bf16[64,2,512]{2,1,0:T(2,128)(2,1)S(1)}, u32[]{:S(2)}, u32[]{:S(2)}) async-start(bf16[64,2,512]{2,1,0:T(2,128)(2,1)} %all_to_all.79), calls=%async_computation.5 | async-start | bytes 262144 | tf_op jit(solution)/shard_map/all_to_all | solution.py:166
  191.4 50.2 %while.61 = (s32[]{:T(128)}, f32[128,256]{0,1:T(8,128)S(1)}, s32[2048]{0:T(1024)S(1)}, s32[128]{0:T(128)S(1)}, bf16[2048,512]{1,0:T(8,128)(2,1)}, /*index=5*/bf1...) while((s32[]{:T(128)}, f32[128,256]{0,1:T(8,128)S(1)}, ...), condition=%wide.region_14.17_spmd.clone, body=%wide.region_13.16_spmd.clone.sunk | while | flops 67879168 | bytes 3006681 | solution.py:149
  241.8 1.5 scatter_custom_fusion.2
  243.2 12.1 %all-to-all-start.6 = ((bf16[64,2,128]{2,1,0:T(2,128)(2,1)}), bf16[64,2,128]{2,1,0:T(2,128)(2,1)S(1)}, u32[]{:S(2)}, u32[]{:S(2)}) async-start(bf16[64,2,128]{2,1,0:T(2,128)(2,1)} %bitcast.5), calls=%async_computation.6 | async-start | bytes 65536 | tf_op jit(solution)/shard_map/all_to_all | solution.py:173
  256.9 9.2 %all-to-all-done.6 = bf16[64,2,128]{2,1,0:T(2,128)(2,1)S(1)} async-done(((bf16[64,2,128]{2,1,0:T(2,128)(2,1)}), bf16[64,2,128]{2,1,0:T(2,128)(2,1)S(1)}, u32[]{:S(2)}, u32[]{:S(2)}) %all-to-all-start.6) | async-done | bytes 32800 | tf_op jit(solution)/shard_map/all_to_all | solution.py:173
  266.2 4.6 %all-to-all-start.7 = ((bf16[64,2,128]{2,1,0:T(2,128)(2,1)}), bf16[64,2,128]{2,1,0:T(2,128)(2,1)S(1)}, u32[]{:S(2)}, u32[]{:S(2)}) async-start(bf16[64,2,128]{2,1,0:T(2,128)(2,1)} %bitcast.7), calls=%async_computation.7 | async-start | bytes 65536 | tf_op jit(solution)/shard_map/all_to_all | solution.py:174
  272.2 9.4 %all-to-all-done.7 = bf16[64,2,128]{2,1,0:T(2,128)(2,1)S(1)} async-done(((bf16[64,2,128]{2,1,0:T(2,128)(2,1)}), bf16[64,2,128]{2,1,0:T(2,128)(2,1)S(1)}, u32[]{:S(2)}, u32[]{:S(2)}) %all-to-all-start.7) | async-done | bytes 32800 | tf_op jit(solution)/shard_map/all_to_all | solution.py:174
  (488 shorter events, 80.2 us)
Async XLA Ops:
  8.8 25.6 %all-to-all-start.1 = ((bf16[64,2,512]{2,1,0:T(2,128)(2,1)}), bf16[64,2,512]{2,1,0:T(2,128)(2,1)S(1)}, u32[]{:S(2)}, u32[]{:S(2)}) async-start(bf16[64,2,512]{2,1,0:T(2,128)(2,1)} %all_to_all.67), calls=%async_computation.1 | async-start | bytes 262144 | tf_op jit(solution)/shard_map/all_to_all | solution.py:35
  22.8 34.3 %copy-start.2 = (s32[1,65]{1,0:T(1,128)S(1)}, s32[1,65]{1,0:T(1,128)}, u32[]{:S(2)}) copy-start(s32[1,65]{1,0:T(1,128)} %param.22) | copy-start | bytes 784
  34.4 16.2 %all-to-all-start.4 = ((bf16[64,2,512]{2,1,0:T(2,128)(2,1)}), bf16[64,2,512]{2,1,0:T(2,128)(2,1)S(1)}, u32[]{:S(2)}, u32[]{:S(2)}) async-start(bf16[64,2,512]{2,1,0:T(2,128)(2,1)} %all_to_all.76), calls=%async_computation.4 | async-start | bytes 262144 | tf_op jit(solution)/shard_map/all_to_all | solution.py:38
  39.0 152.4 %all-gather.3.cloned.1.call-start = ((), (), s32[]{:S(2)}) async-start(), calls=%async_computation.8 | async-start | bytes 2228224 | tf_op jit(solution)/shard_map/all_gather | solution.py:121
  52.3 84.0 %copy-start.1 = (bf16[128,512]{1,0:T(8,128)(2,1)S(1)}, bf16[128,512]{1,0:T(8,128)(2,1)}, u32[]{:S(2)}) copy-start(bf16[128,512]{1,0:T(8,128)(2,1)} %get-tuple-element.973) | copy-start | bytes 393220
  52.3 15.5 %all-to-all-start.2 = ((bf16[64,2,128]{2,1,0:T(2,128)(2,1)}), bf16[64,2,128]{2,1,0:T(2,128)(2,1)S(1)}, u32[]{:S(2)}, u32[]{:S(2)}) async-start(bf16[64,2,128]{2,1,0:T(2,128)(2,1)} %bitcast.3), calls=%async_computation.2 | async-start | bytes 65536 | tf_op jit(solution)/shard_map/all_to_all | solution.py:37
  67.8 15.4 %all-to-all-start = ((bf16[64,2,128]{2,1,0:T(2,128)(2,1)}), bf16[64,2,128]{2,1,0:T(2,128)(2,1)S(1)}, u32[]{:S(2)}, u32[]{:S(2)}) async-start(bf16[64,2,128]{2,1,0:T(2,128)(2,1)} %bitcast.1), calls=%async_computation | async-start | bytes 65536 | tf_op jit(solution)/shard_map/all_to_all | solution.py:36
  72.4 119.0 %all-gather.5.cloned.1.call-start = ((), (), s32[]{:S(2)}) async-start(), calls=%async_computation.9 | async-start | bytes 2228224 | tf_op jit(solution)/shard_map/all_gather | solution.py:122
  136.4 5.3 %copy-start = (bf16[128,512]{1,0:T(8,128)(2,1)S(1)}, bf16[128,512]{1,0:T(8,128)(2,1)}, u32[]{:S(2)}) copy-start(bf16[128,512]{1,0:T(8,128)(2,1)} %get-tuple-element.974) | copy-start | bytes 393220
  149.3 29.8 %all-to-all-start.3 = ((bf16[64,2,512]{2,1,0:T(2,128)(2,1)}), bf16[64,2,512]{2,1,0:T(2,128)(2,1)S(1)}, u32[]{:S(2)}, u32[]{:S(2)}) async-start(bf16[64,2,512]{2,1,0:T(2,128)(2,1)} %all_to_all.73), calls=%async_computation.3 | async-start | bytes 262144 | tf_op jit(solution)/shard_map/all_to_all | solution.py:159
  179.1 64.1 %all-to-all-start.5 = ((bf16[64,2,512]{2,1,0:T(2,128)(2,1)}), bf16[64,2,512]{2,1,0:T(2,128)(2,1)S(1)}, u32[]{:S(2)}, u32[]{:S(2)}) async-start(bf16[64,2,512]{2,1,0:T(2,128)(2,1)} %all_to_all.79), calls=%async_computation.5 | async-start | bytes 262144 | tf_op jit(solution)/shard_map/all_to_all | solution.py:166
  243.2 22.9 %all-to-all-start.6 = ((bf16[64,2,128]{2,1,0:T(2,128)(2,1)}), bf16[64,2,128]{2,1,0:T(2,128)(2,1)S(1)}, u32[]{:S(2)}, u32[]{:S(2)}) async-start(bf16[64,2,128]{2,1,0:T(2,128)(2,1)} %bitcast.5), calls=%async_computation.6 | async-start | bytes 65536 | tf_op jit(solution)/shard_map/all_to_all | solution.py:173
  266.2 15.4 %all-to-all-start.7 = ((bf16[64,2,128]{2,1,0:T(2,128)(2,1)}), bf16[64,2,128]{2,1,0:T(2,128)(2,1)S(1)}, u32[]{:S(2)}, u32[]{:S(2)}) async-start(bf16[64,2,128]{2,1,0:T(2,128)(2,1)} %bitcast.7), calls=%async_computation.7 | async-start | bytes 65536 | tf_op jit(solution)/shard_map/all_to_all | solution.py:174
Sparse Core Ops, SparseCore 0:
  52.4 50.9 all-gather.2
  136.5 33.8 all-gather.4
where the time goes:
time: 291 us; the launch traced here: 290 us
  blocking collectives  68.2 us (23%)
  starting transfers between devices  61.8 us (21%)
  waiting for transfers between devices  58.1 us (20%)
  local copies, waits for them, and re-layouts  56.5 us (19%)
  matrix products  23.5 us (8%)
  between operations  14.4 us (5%)
  other arithmetic  4.82 us (2%)
    all_gather x1, blocking collectives, local(): lax.all_gather(key_local, 'ctx', axis=0, tiled=True)  36.4 us
    all_gather x1, blocking collectives, local(): group_stats = lax.all_gather(own_stats, 'ctx', axis=0, tiled=True)  16 us
    all_gather x1, blocking collectives, local(): lax.all_gather(value_local, 'ctx', axis=0, tiled=True)  15.9 us
    dynamic_slice x16, local copies, waits for them, and re-layouts, piece_step(): lax.dynamic_slice_in_dim(grad_piece, offset, piece_rows)  15.9 us
    all_to_all x1, starting transfers between devices, local(): lax.all_to_all(queries, 'dp', split_axis=0, concat_axis=0, tiled=True)  14 us
    all_to_all x1, starting transfers between devices, local(): lax.all_to_all(placed(query_grad_low.reshape(row_count, head_count * head...  12.2 us
    all_to_all x1, starting transfers between devices, local(): lax.all_to_all(placed(key_grad_low), 'dp', split_axis=0, concat_axis=0, t...  12.1 us
    all_to_all x1, waiting for transfers between devices, local(): lax.all_to_all(values, 'dp', split_axis=0, concat_axis=0, tiled=True)  10.2 us
  transfers between devices with their start and end apart: 10, of which 6 were waited for; matrix products, arithmetic and copies ran while one was open for 26% of the time, Pallas kernels for 0%

commit v1 on v0

v1 whole, which is shorter than its diff:
```python
import functools
import math

import jax
import jax.numpy as jnp
from jax import lax
from jax.experimental import pallas as pl
from jax.experimental.pallas import tpu as pltpu
from jax.sharding import PartitionSpec as P

MESH = pl.DeviceIdType.MESH
NEG = -1e30
F32 = jnp.float32
BF16 = jnp.bfloat16


def mm(left, right):
    return jnp.dot(left, right, preferred_element_type=F32)


def mm_nt(left, right):
    return lax.dot_general(left, right, (((1,), (1,)), ((), ())), preferred_element_type=F32)


def iota(shape, dim):
    return lax.broadcasted_iota(jnp.int32, shape, dim)


def far_first(n):
    order = sorted(range(1, n), key=lambda k: -min(k, n - k))
    return order


def kernel(
    ny, nx, nz, heads,
    q_hbm, k_hbm, v_hbm, g_hbm, lens_ref, slot_ref,
    o_out, dq_out, dk_out, dv_out,
    in_kv, in_qg, y_kv, y_qg, x_kv, x_qg, kv_all, qg,
    qf, gf, gt, s_all, dp_all, bias, lens_pad, m_row, l_row, o_t, dq_t,
    x_out, r_out, z_out, f_out, part, sib_part, comb, acc, z_kv, f_kv,
    in_sem, y_send, y_recv, xz_send, xz_recv, qg_send, qg_recv, fwd_send, fwd_recv,
    xo_send, xo_recv, yo_send, yo_recv, yk_send, yk_recv, part_send, part_recv, acc_send, acc_recv,
    ready,
):
    tok = in_kv.shape[0]
    dh = k_hbm.shape[1]
    wide = heads * dh
    peer = tok // (ny * nx)
    blk = tok // ny
    scale = dh ** -0.5
    dp = lax.axis_index("dp")
    ctx = lax.axis_index("ctx")
    y, x = dp // nx, dp % nx
    z, core = ctx // 2, ctx % 2
    sibling = (dp, z * 2 + 1 - core)

    def at(yy, xx, zz):
        return (yy * nx + xx, zz * 2 + core)

    def rows(i):
        return pl.ds(pl.multiple_of(i * blk, blk), blk)

    def remote(src, dst, send, recv, dev):
        return pltpu.make_async_remote_copy(
            src_ref=src, dst_ref=dst, send_sem=send, recv_sem=recv, device_id=dev, device_id_type=MESH
        )

    def drain(ref, sem):
        pltpu.make_async_copy(ref, ref, sem).wait()

    loads = [
        pltpu.make_async_copy(k_hbm, in_kv.at[:, pl.ds(0, dh)], in_sem.at[0]),
        pltpu.make_async_copy(v_hbm, in_kv.at[:, pl.ds(dh, dh)], in_sem.at[1]),
        pltpu.make_async_copy(q_hbm, in_qg.at[:, pl.ds(0, wide)], in_sem.at[2]),
        pltpu.make_async_copy(g_hbm, in_qg.at[:, pl.ds(wide, wide)], in_sem.at[3]),
    ]
    for load in loads:
        load.start()

    barrier = pltpu.get_barrier_semaphore()
    for k in far_first(ny):
        pl.semaphore_signal(barrier, inc=1, device_id=at((y + k) % ny, x, z), device_id_type=MESH)
    for k in far_first(nx):
        pl.semaphore_signal(barrier, inc=1, device_id=at(y, (x + k) % nx, z), device_id_type=MESH)
    for k in far_first(nz):
        pl.semaphore_signal(barrier, inc=1, device_id=at(y, x, (z + k) % nz), device_id_type=MESH)
    pl.semaphore_signal(barrier, inc=1, device_id=sibling, device_id_type=MESH)
    for load in loads:
        load.wait()
    pl.semaphore_wait(barrier, ny + nx + nz - 2)

    for i, (src, dst) in enumerate(((in_kv, y_kv), (in_qg, y_qg))):
        for k in far_first(ny):
            t = (y + k) % ny
            remote(src.at[rows(t)], dst.at[rows(y)], y_send.at[i], y_recv.at[i], at(t, x, z)).start()
        dst[rows(y), :] = src[rows(y), :]
    for k in far_first(nx):
        pl.semaphore_signal(ready, inc=1, device_id=at(y, (x + k) % nx, z), device_id_type=MESH)

    row_i, col_i = iota((tok, tok), 0), iota((tok, tok), 1)
    swapped = (row_i // peer % nx) * blk + (row_i // blk) * peer + row_i % peer
    regroup = (swapped == col_i).astype(BF16)
    eye = (row_i == col_i).astype(F32)
    eye_low = eye.astype(BF16)

    slot = slot_ref[...]
    arrived = (slot // peer % nx) * blk + (slot // blk) * peer + slot % peer
    pos_col = jnp.sum(jnp.where(row_i == arrived, col_i.astype(F32), 0.0), axis=1, keepdims=True)
    pos_row = jnp.sum(eye * pos_col, axis=0, keepdims=True)
    lens_pad[...] = jnp.zeros_like(lens_pad)
    lens_pad[:, pl.ds(0, lens_ref.shape[1])] = lens_ref[...].astype(F32)
    lens = lens_pad[...]
    pad = lens.shape[1]
    below = iota((pad, pad), 1) <= iota((pad, pad), 0)
    ends_col = jnp.sum(jnp.where(below, lens, 0.0), axis=1, keepdims=True)
    first = (ctx * tok).astype(F32)
    doc_row = jnp.sum((ends_col <= pos_row + first).astype(F32), axis=0, keepdims=True)
    doc_col = jnp.sum(eye * doc_row, axis=1, keepdims=True)
    seen = (doc_col == doc_row) & (pos_col <= pos_row)
    own = jnp.where(seen, 0.0, NEG)
    later = jnp.where(lens[:, :1] >= first + tok, 0.0, NEG) + jnp.zeros((tok, tok), F32)
    bias[0, pl.ds(0, tok), :] = jnp.where(core == 0, own, later)
    bias[0, pl.ds(tok, tok), :] = jnp.where(core == 0, NEG, own)
    bias[1, pl.ds(0, tok), :] = later
    bias[1, pl.ds(tok, tok), :] = later

    drain(y_kv.at[pl.ds(0, tok - blk)], y_recv.at[0])
    x_kv[...] = mm(regroup, y_kv[...]).astype(BF16)
    pl.semaphore_wait(ready, nx - 1)

    def offset(t):
        return jnp.where(t % 2 == 1, (t + 1) // 2, (nz - t // 2) % nz)

    def kv_out(i, carry):
        o = offset(nz - 1 - i)

        @pl.when(z + o < nz)
        def _():
            for k in range(nx):
                t = (x + k) % nx

                def send():
                    remote(
                        x_kv.at[rows(t)], kv_all.at[ctx, rows(x)], xz_send.at[z + o], xz_recv.at[z], at(y, t, z + o)
                    ).start()

                if k == 0:
                    pl.when(o > 0)(send)
                else:
                    send()

        return carry

    lax.fori_loop(0, nz, kv_out, 0)
    kv_all[ctx, rows(x), :] = x_kv[rows(x), :]

    drain(y_qg.at[pl.ds(0, tok - blk)], y_recv.at[1])
    x_qg[...] = mm(regroup, y_qg[...]).astype(BF16)
    for k in far_first(nx):
        t = (x + k) % nx
        remote(x_qg.at[rows(t)], qg.at[rows(x)], qg_send, qg_recv, at(y, t, z)).start()
    qg[rows(x), :] = x_qg[rows(x), :]

    def kv_forward(zz):
        here = zz * 2 + core

        @pl.when(zz == z)
        def _():
            drain(x_kv.at[pl.ds(0, tok - blk)], xz_recv.at[zz])

        @pl.when(zz != z)
        def _():
            drain(x_kv, xz_recv.at[zz])

        remote(kv_all.at[here], kv_all.at[here], fwd_send.at[zz], fwd_recv.at[zz], sibling).start()

    kv_forward(z)
    m_row[...] = jnp.full_like(m_row, NEG)
    l_row[...] = jnp.zeros_like(l_row)
    o_t[...] = jnp.zeros_like(o_t)
    dq_t[...] = jnp.zeros_like(dq_t)

    drain(qg.at[pl.ds(0, tok - blk)], qg_recv)
    for h in range(heads):
        cols = pl.ds(h * dh, dh)
        grad = qg[:, pl.ds(wide + h * dh, dh)]
        qf[pl.ds(h * tok, tok), :] = qg[:, cols]
        gf[pl.ds(h * tok, tok), :] = grad
        gt[:, pl.ds(h * tok, tok)] = mm_nt(eye_low, grad)

    def pair(zz):
        both = kv_all[pl.ds(zz * 2, 2)].reshape(2 * tok, 2 * dh)
        return both[:, :dh], both[:, dh:]

    def forward(t, carry):
        o = offset(t)
        nxt = offset(t + 1)

        @pl.when((t + 1 < nz) & (z >= nxt))
        def _():
            kv_forward(z - nxt)

        @pl.when(z >= o)
        def _():
            zz = z - o
            drain(x_kv, fwd_recv.at[zz])
            key, value = pair(zz)
            shift = bias[jnp.minimum(o, 1)]
            score = mm_nt(key, qf[...]) * scale + jnp.concatenate([shift] * heads, axis=1)
            s_all[zz] = score
            dp_all[zz] = mm_nt(value, gf[...])
            old = m_row[...]
            new = jnp.maximum(old, jnp.max(score, axis=0, keepdims=True))
            weight = jnp.exp(score - new)
            fade = jnp.exp(old - new)
            m_row[...] = new
            l_row[...] = l_row[...] * fade + jnp.sum(weight, axis=0, keepdims=True)
            value_t = mm_nt(eye_low, value).astype(BF16)
            o_t[...] = o_t[...] * fade + mm(value_t, weight.astype(BF16))

        return carry

    lax.fori_loop(0, nz, forward, 0)

    attended_t = (o_t[...] * (1.0 / l_row[...])).astype(BF16)
    delta = jnp.sum(gt[...] * attended_t.astype(F32), axis=0, keepdims=True)
    log_total = m_row[...] + jnp.log(l_row[...])

    def send_x(i, value_t):
        for h in range(heads):
            x_out[i, :, pl.ds(h * dh, dh)] = mm_nt(eye_low, value_t[:, h * tok : (h + 1) * tok]).astype(BF16)
        for k in far_first(nx):
            t = (x + k) % nx
            remote(x_out.at[i, rows(t)], r_out.at[i, rows(x)], xo_send.at[i], xo_recv.at[i], at(y, t, z)).start()
        r_out[i, rows(x), :] = x_out[i, rows(x), :]

    def send_y(i):
        drain(r_out.at[i, pl.ds(0, tok - blk)], xo_recv.at[i])
        z_out[i] = mm(regroup, r_out[i]).astype(BF16)
        for k in far_first(ny):
            t = (y + k) % ny
            remote(z_out.at[i, rows(t)], f_out.at[i, rows(y)], yo_send.at[i], yo_recv.at[i], at(t, x, z)).start()
        f_out[i, rows(y), :] = z_out[i, rows(y), :]

    send_x(0, attended_t)

    def share(zz):
        drain(x_kv, part_recv.at[zz])
        comb[zz] = (part[zz, core].astype(F32) + sib_part[zz].astype(F32)).astype(BF16)
        for k in range(nx):
            t = (x + k) % nx

            def send():
                remote(
                    comb.at[zz, rows(t)], acc.at[z, rows(x)], acc_send.at[zz], acc_recv.at[z], at(y, t, zz)
                ).start()

            if k == 0:
                pl.when(zz < z)(send)
            else:
                send()

    def backward(i, carry):
        t = nz - 1 - i
        o = offset(t)
        last = offset(t + 1)

        @pl.when(z >= o)
        def _():
            zz = z - o
            key, value = pair(zz)
            prob = jnp.exp(s_all[zz] - log_total)
            score_grad = (prob * (dp_all[zz] - delta)).astype(BF16)
            key_t = mm_nt(eye_low, key).astype(BF16)
            value_part = mm(prob.astype(BF16), gf[...])
            key_part = mm(score_grad, qf[...]) * scale
            dq_t[...] += mm(key_t, score_grad)
            for b in range(2):
                part[zz, b, :, pl.ds(0, dh)] = key_part[b * tok : (b + 1) * tok].astype(BF16)
                part[zz, b, :, pl.ds(dh, dh)] = value_part[b * tok : (b + 1) * tok].astype(BF16)
            remote(part.at[zz, 1 - core], sib_part.at[zz], part_send.at[zz], part_recv.at[zz], sibling).start()

        @pl.when((t + 1 < nz) & (z >= last))
        def _():
            share(z - last)

        return carry

    lax.fori_loop(0, nz, backward, 0)
    send_x(1, (dq_t[...] * scale).astype(BF16))
    share(z)
    acc[z, rows(x), :] = comb[z, rows(x), :]
    send_y(0)

    total = jnp.zeros((tok, 2 * dh), F32)
    y_kv_sum = y_kv
    for zz in range(nz):

        @pl.when(zz > z)
        def _():
            drain(x_kv, acc_recv.at[zz])

        @pl.when(zz == z)
        def _():
            drain(x_kv.at[pl.ds(0, tok - blk)], acc_recv.at[zz])

        @pl.when(zz < z)
        def _():
            acc[zz] = jnp.zeros((tok, 2 * dh), BF16)

        total = total + acc[zz].astype(F32)
    z_kv[...] = mm(regroup, total.astype(BF16)).astype(BF16)
    for k in far_first(ny):
        t = (y + k) % ny
        remote(z_kv.at[rows(t)], f_kv.at[rows(y)], yk_send, yk_recv, at(t, x, z)).start()
    f_kv[rows(y), :] = z_kv[rows(y), :]
    send_y(1)

    for i, ref in enumerate((in_kv, in_qg)):
        drain(ref.at[pl.ds(0, tok - blk)], y_send.at[i])
    drain(x_qg.at[pl.ds(0, tok - blk)], qg_send)
    for zz in range(nz):

        @pl.when(zz > z)
        def _():
            drain(x_kv, xz_send.at[zz])

        @pl.when(zz == z)
        def _():
            drain(x_kv.at[pl.ds(0, tok - blk)], xz_send.at[zz])
            drain(x_kv.at[pl.ds(0, tok - blk)], acc_send.at[zz])

        @pl.when(zz < z)
        def _():
            drain(x_kv, acc_send.at[zz])

        @pl.when(zz <= z)
        def _():
            drain(x_kv, fwd_send.at[zz])
            drain(x_kv, part_send.at[zz])

    for i in range(2):
        drain(x_out.at[i, pl.ds(0, tok - blk)], xo_send.at[i])
        drain(z_out.at[i, pl.ds(0, tok - blk)], yo_send.at[i])
    drain(z_kv.at[pl.ds(0, tok - blk)], yk_send)
    drain(f_out.at[0, pl.ds(0, tok - blk)], yo_recv.at[0])
    o_out[...] = f_out[0]
    drain(f_kv.at[pl.ds(0, tok - blk)], yk_recv)
    dk_out[...] = f_kv[:, :dh]
    dv_out[...] = f_kv[:, dh:]
    drain(f_out.at[1, pl.ds(0, tok - blk)], yo_recv.at[1])
    dq_out[...] = f_out[1]


def local(ny, nx, nz, queries, keys, values, out_grad, doc_lengths, source_slot):
    tok, dh = keys.shape
    wide = queries.shape[1]
    heads = wide // dh
    flat = heads * tok
    pad = -(-doc_lengths.shape[1] // 128) * 128
    dma = pltpu.SemaphoreType.DMA
    hbm = pl.BlockSpec(memory_space=pltpu.MemorySpace.HBM)
    vmem = pl.BlockSpec(memory_space=pltpu.VMEM)
    low = lambda *shape: pltpu.VMEM(shape, BF16)
    full = lambda *shape: pltpu.VMEM(shape, F32)
    return pl.pallas_call(
        functools.partial(kernel, ny, nx, nz, heads),
        out_shape=(
            jax.ShapeDtypeStruct((tok, wide), BF16),
            jax.ShapeDtypeStruct((tok, wide), BF16),
            jax.ShapeDtypeStruct((tok, dh), BF16),
            jax.ShapeDtypeStruct((tok, dh), BF16),
        ),
        in_specs=[hbm] * 4 + [vmem] * 2,
        out_specs=[vmem] * 4,
        scratch_shapes=[
            low(tok, 2 * dh), low(tok, 2 * wide),
            low(tok, 2 * dh), low(tok, 2 * wide),
            low(tok, 2 * dh), low(tok, 2 * wide),
            low(2 * nz, tok, 2 * dh), low(tok, 2 * wide),
            low(flat, dh), low(flat, dh), full(dh, flat),
            full(nz, 2 * tok, flat), full(nz, 2 * tok, flat),
            full(2, 2 * tok, tok), full(1, pad),
            full(1, flat), full(1, flat), full(dh, flat), full(dh, flat),
            low(2, tok, wide), low(2, tok, wide), low(2, tok, wide), low(2, tok, wide),
            low(nz, 2, tok, 2 * dh), low(nz, tok, 2 * dh), low(nz, tok, 2 * dh),
            low(nz, tok, 2 * dh), low(tok, 2 * dh), low(tok, 2 * dh),
            dma((4,)), dma((2,)), dma((2,)), dma((nz,)), dma((nz,)), dma(()), dma(()), dma((nz,)), dma((nz,)),
            dma((2,)), dma((2,)), dma((2,)), dma((2,)), dma(()), dma(()), dma((nz,)), dma((nz,)), dma((nz,)), dma((nz,)),
            pltpu.SemaphoreType.REGULAR,
        ],
        compiler_params=pltpu.CompilerParams(collective_id=0, has_side_effects=True),
        name="packed_attention",
    )(queries, keys, values, out_grad, doc_lengths, source_slot.reshape(1, tok))


def solution(mesh):
    side = math.isqrt(mesh.shape["dp"])
    placed = (
        P(("dp", "ctx"), None),
        P(("dp", "ctx"), None),
        P(("dp", "ctx"), None),
        P(("dp", "ctx"), None),
        P("dp", None),
        P(("dp", "ctx")),
    )
    return jax.shard_map(
        functools.partial(local, side, side, mesh.shape["ctx"] // 2),
        mesh=mesh,
        in_specs=placed,
        out_specs=(
            P(("dp", "ctx"), None),
            P(("dp", "ctx"), None),
            P(("dp", "ctx"), None),
            P(("dp", "ctx"), None),
        ),
        check_vma=False,
    )
```

time: 291 us -> 75.5 us (0.26)
  Pallas kernels: 0 us -> 70.6 us
  blocking collectives: 68.2 us -> 0 us
  starting transfers between devices: 61.8 us -> 0 us
  waiting for transfers between devices: 58.1 us -> 0 us
  local copies, waits for them, and re-layouts: 56.5 us -> 3.75 us
  matrix products: 23.5 us -> 0 us
  between operations: 14.4 us -> 0.65 us
  other arithmetic: 4.82 us -> 0 us
    pallas_call x0 -> x1, Pallas kernels: none -> 70.6 us  [local(): pl.pallas_call(functools.partial(kernel, ny, nx, nz, heads), out_shape=(j...]
    all_gather x3 -> x0, blocking collectives: 68.2 us -> none  [the longest x1 36.4 us: local(): lax.all_gather(key_local, 'ctx', axis=0, tiled=True)]
    all_to_all x8 -> x0, starting transfers between devices: 61.7 us -> none  [the longest x1 14 us: local(): lax.all_to_all(queries, 'dp', split_axis=0, concat_axis=0, tiled=True)]
    all_to_all x8 -> x0, waiting for transfers between devices: 58 us -> none  [the longest x1 10.2 us: local(): lax.all_to_all(values, 'dp', split_axis=0, concat_axis=0, tiled=True)]
    dot_general x64 -> x0, matrix products: 23.5 us -> none  [the longest x32 9.66 us: contract_rows(): lax.dot_general(left, right, (((0,), (0,)), ((), ())), preferred_element_...]
    dynamic_slice x73 -> x0, local copies, waits for them, and re-layouts: 19.2 us -> none  [the longest x16 15.9 us: piece_step(): lax.dynamic_slice_in_dim(grad_piece, offset, piece_rows)]
    all_to_all x8 -> x0, local copies, waits for them, and re-layouts: 6.19 us -> none  [the longest x2 1.68 us: local(): lax.all_to_all(out_grad, 'dp', split_axis=0, concat_axis=0, tiled=True)]
    scatter x4 -> x0, local copies, waits for them, and re-layouts: 5.07 us -> none  [placed(): return jnp.zeros_like(computed).at[source_slot].set(computed)]
  transfers between devices with their start and end apart: 10 -> 0, of which waited for: 6 -> 0; matrix products, arithmetic and copies ran while one was open for 26% -> 0% of each run, Pallas kernels for 0% -> 0%
where the time goes in v1:
time: 75.5 us; the launch traced here: 75 us
  Pallas kernels  70.6 us (94%)
  local copies, waits for them, and re-layouts  3.75 us (5%)
    pallas_call x1, Pallas kernels, local(): pl.pallas_call(functools.partial(kernel, ny, nx, nz, heads), out_shape=(j...  70.6 us
    unnamed x10, local copies, waits for them, and re-layouts  3.75 us

profile of v1, /device:TPU:1, one launch (start us, length us, event | category | flops | bytes accessed | tf_op | source)
XLA Modules:
  0.0 75.0 jit_solution(13206992370297155883)
XLA Ops:
  0.6 70.6 %packed_attention.1 = (bf16[128,512]{1,0:T(8,128)(2,1)}, bf16[128,512]{1,0:T(8,128)(2,1)}, bf16[128,128]{1,0:T(8,128)(2,1)}, bf16[128,128]{1,0:T(8,128)(2,1)}) custom-call(bf16[128,512]{1,0:T(8,128)(2,1)} %q_hbm.1, bf16[128,128]{1,0:T(8,128)(2,1)} %k_hbm.1, bf16[128,128]{1,0:T(8,128)(2,1)} %v_hbm.1, bf16[128,512]{1,0:T(8,128)(2,1)} %g_hbm.1, ...), custom_call_target="tpu_custom_call" | custom-call | tf_op jit(solution)/shard_map/packed_attention/pallas_call | solution.py:366
  71.3 0.0 copy-start
  71.3 1.6 %copy.14 = bf16[128,512]{1,0:T(8,128)(2,1)} copy(bf16[128,512]{1,0:T(8,128)(2,1)} %get-tuple-element.8) | data formatting | bytes 262144
  72.9 0.0 copy-done
  72.9 0.0 copy-start.2
  72.9 0.7 copy.15
  73.5 0.1 copy-done.2
  73.6 0.0 copy-start.1
  73.6 0.6 copy.16
  74.2 0.2 copy-done.1
  74.4 0.6 copy.17
Async XLA Ops:
  71.3 1.6 %copy-start = (bf16[128,512]{1,0:T(8,128)(2,1)S(1)}, bf16[128,512]{1,0:T(8,128)(2,1)}, u32[]{:S(2)}) copy-start(bf16[128,512]{1,0:T(8,128)(2,1)} %get-tuple-element.9) | copy-start | bytes 393220
  72.9 0.8 %copy-start.2 = (bf16[128,128]{1,0:T(8,128)(2,1)S(1)}, bf16[128,128]{1,0:T(8,128)(2,1)}, u32[]{:S(2)}) copy-start(bf16[128,128]{1,0:T(8,128)(2,1)} %get-tuple-element.10) | copy-start | bytes 98308
  73.6 0.8 %copy-start.1 = (bf16[128,128]{1,0:T(8,128)(2,1)S(1)}, bf16[128,128]{1,0:T(8,128)(2,1)}, u32[]{:S(2)}) copy-start(bf16[128,128]{1,0:T(8,128)(2,1)} %get-tuple-element.11) | copy-start | bytes 98308

commit v2 on v1

v2 whole, which is shorter than its diff:
```python
import functools
import math

import jax
import jax.numpy as jnp
from jax import lax
from jax.experimental import pallas as pl
from jax.experimental.pallas import tpu as pltpu
from jax.sharding import PartitionSpec as P

MESH = pl.DeviceIdType.MESH
NEG = -1e30
F32 = jnp.float32
BF16 = jnp.bfloat16


def OUT(*shape):
    return pltpu.VMEM(shape, BF16)


def mm(left, right):
    return jnp.dot(left, right, preferred_element_type=F32)


def mm_nt(left, right):
    return lax.dot_general(left, right, (((1,), (1,)), ((), ())), preferred_element_type=F32)


def iota(shape, dim):
    return lax.broadcasted_iota(jnp.int32, shape, dim)


def far_first(n):
    order = sorted(range(1, n), key=lambda k: -min(k, n - k))
    return order


def kernel(
    ny, nx, nz, heads,
    q_hbm, k_hbm, v_hbm, g_hbm, lens_hbm, slot_hbm,
    f_o, f_dq, f_kv,
    in_kv, in_q, in_g, lens_in, slot_in, y_kv, y_q, x_g, s_kv, s_q, s_g0, s_g, kv_all, q_all, g_all,
    qf, gf, gt, s_all, dp_all, bias, lens_pad, m_row, l_row, o_t, dq_t,
    x_out, r_out, z_out, part, sib_part, comb, acc, s_dkv, r_dkv, z_dkv,
    in_sem, a_send, a_recv, b_send, b_recv, z_send, z_recv, fwd_send, fwd_recv,
    xo_send, xo_recv, yo_send, yo_recv, part_send, part_recv, acc_send, acc_recv,
):
    tok = in_kv.shape[0]
    dh = k_hbm.shape[1]
    wide = heads * dh
    peer = tok // (ny * nx)
    blk = tok // ny
    scale = dh ** -0.5
    dp = lax.axis_index("dp")
    ctx = lax.axis_index("ctx")
    y, x = dp // nx, dp % nx
    z, core = ctx // 2, ctx % 2
    sibling = (dp, z * 2 + 1 - core)

    def at(yy, xx, zz):
        return (yy * nx + xx, zz * 2 + core)

    def rows(i):
        return pl.ds(pl.multiple_of(i * blk, blk), blk)

    def remote(src, dst, send, recv, dev):
        return pltpu.make_async_remote_copy(
            src_ref=src, dst_ref=dst, send_sem=send, recv_sem=recv, device_id=dev, device_id_type=MESH
        )

    def drain(ref, sem):
        pltpu.make_async_copy(ref, ref, sem).wait()

    def others(ref):
        return ref.at[pl.ds(0, tok - blk)]

    def along(axis, src, dst, send, recv):
        me = y if axis == "y" else x
        n = ny if axis == "y" else nx
        for k in far_first(n):
            t = (me + k) % n
            dev = at(t, x, z) if axis == "y" else at(y, t, z)
            remote(src.at[rows(t)], dst.at[rows(me)], send, recv, dev).start()
        dst[rows(me), :] = src[rows(me), :]

    barrier = pltpu.get_barrier_semaphore()
    for k in far_first(ny):
        pl.semaphore_signal(barrier, inc=1, device_id=at((y + k) % ny, x, z), device_id_type=MESH)
    for k in far_first(nx):
        pl.semaphore_signal(barrier, inc=1, device_id=at(y, (x + k) % nx, z), device_id_type=MESH)
    for k in far_first(nz):
        pl.semaphore_signal(barrier, inc=1, device_id=at(y, x, (z + k) % nz), device_id_type=MESH)
    pl.semaphore_signal(barrier, inc=1, device_id=sibling, device_id_type=MESH)

    loads = [
        pltpu.make_async_copy(g_hbm, in_g, in_sem.at[0]),
        pltpu.make_async_copy(k_hbm, in_kv.at[:, pl.ds(0, dh)], in_sem.at[1]),
        pltpu.make_async_copy(v_hbm, in_kv.at[:, pl.ds(dh, dh)], in_sem.at[2]),
        pltpu.make_async_copy(q_hbm, in_q, in_sem.at[3]),
        pltpu.make_async_copy(lens_hbm, lens_in, in_sem.at[4]),
        pltpu.make_async_copy(slot_hbm, slot_in, in_sem.at[5]),
    ]
    for load in loads:
        load.start()

    row_i, col_i = iota((tok, tok), 0), iota((tok, tok), 1)
    swapped = (row_i // peer % nx) * blk + (row_i // blk) * peer + row_i % peer
    regroup = (swapped == col_i).astype(BF16)
    eye = (row_i == col_i).astype(F32)
    eye_low = eye.astype(BF16)

    loads[0].wait()
    s_g0[...] = mm(regroup, in_g[...]).astype(BF16)
    for load in loads[1:]:
        load.wait()
    pl.semaphore_wait(barrier, ny + nx + nz - 2)

    along("y", in_kv, y_kv, a_send.at[0], a_recv.at[0])
    along("y", in_q, y_q, a_send.at[1], a_recv.at[1])
    along("x", s_g0, x_g, a_send.at[2], a_recv.at[2])

    slot = slot_in[...]
    arrived = (slot // peer % nx) * blk + (slot // blk) * peer + slot % peer
    pos_col = jnp.sum(jnp.where(row_i == arrived, col_i.astype(F32), 0.0), axis=1, keepdims=True)
    pos_row = jnp.sum(eye * pos_col, axis=0, keepdims=True)
    lens_pad[...] = jnp.zeros_like(lens_pad)
    lens_pad[:, pl.ds(0, lens_in.shape[1])] = lens_in[...].astype(F32)
    lens = lens_pad[...]
    pad = lens.shape[1]
    below = iota((pad, pad), 1) <= iota((pad, pad), 0)
    ends_col = jnp.sum(jnp.where(below, lens, 0.0), axis=1, keepdims=True)
    first = (ctx * tok).astype(F32)
    doc_row = jnp.sum((ends_col <= pos_row + first).astype(F32), axis=0, keepdims=True)
    doc_col = jnp.sum(eye * doc_row, axis=1, keepdims=True)
    seen = (doc_col == doc_row) & (pos_col <= pos_row)
    own = jnp.where(seen, 0.0, NEG)
    later = jnp.where(lens[:, :1] >= first + tok, 0.0, NEG) + jnp.zeros((tok, tok), F32)
    bias[0, pl.ds(0, tok), :] = jnp.where(core == 0, own, later)
    bias[0, pl.ds(tok, tok), :] = jnp.where(core == 0, NEG, own)
    bias[1, pl.ds(0, tok), :] = later
    bias[1, pl.ds(tok, tok), :] = later
    m_row[...] = jnp.full_like(m_row, NEG)
    l_row[...] = jnp.zeros_like(l_row)
    o_t[...] = jnp.zeros_like(o_t)
    dq_t[...] = jnp.zeros_like(dq_t)

    drain(others(y_kv), a_recv.at[0])
    s_kv[...] = mm(regroup, y_kv[...]).astype(BF16)
    along("x", s_kv, kv_all.at[ctx], b_send.at[0], b_recv.at[0])
    drain(others(x_g), a_recv.at[2])
    s_g[...] = mm(regroup, x_g[...]).astype(BF16)
    along("y", s_g, g_all, b_send.at[2], b_recv.at[2])
    drain(others(y_q), a_recv.at[1])
    s_q[...] = mm(regroup, y_q[...]).astype(BF16)
    along("x", s_q, q_all, b_send.at[1], b_recv.at[1])

    def offset(t):
        return jnp.where(t % 2 == 1, (t + 1) // 2, (nz - t // 2) % nz)

    drain(others(s_kv), b_recv.at[0])

    def to_core(zz):
        here = kv_all.at[zz * 2 + core]
        remote(here, here, fwd_send.at[zz], fwd_recv.at[zz], sibling).start()

    def kv_out(i, carry):
        o = offset(nz - 1 - i)

        @pl.when(z + o < nz)
        def _():
            remote(kv_all.at[ctx], kv_all.at[ctx], z_send.at[z + o], z_recv.at[z], at(y, x, z + o)).start()

        return carry

    lax.fori_loop(0, nz - 1, kv_out, 0)
    to_core(z)

    drain(others(q_all), b_recv.at[1])
    for h in range(heads):
        qf[pl.ds(h * tok, tok), :] = q_all[:, pl.ds(h * dh, dh)]
    drain(others(g_all), b_recv.at[2])
    for h in range(heads):
        grad = mm(regroup, g_all[:, pl.ds(h * dh, dh)]).astype(BF16)
        gf[pl.ds(h * tok, tok), :] = grad
        gt[:, pl.ds(h * tok, tok)] = mm_nt(eye_low, grad)

    def pair(zz):
        both = kv_all[pl.ds(zz * 2, 2)].reshape(2 * tok, 2 * dh)
        return both[:, :dh], both[:, dh:]

    def forward(t, carry):
        o = offset(t)
        nxt = offset(t + 1)

        @pl.when((t + 1 < nz) & (z >= nxt))
        def _():
            drain(s_kv, z_recv.at[z - nxt])
            to_core(z - nxt)

        @pl.when(z >= o)
        def _():
            zz = z - o
            drain(s_kv, fwd_recv.at[zz])
            key, value = pair(zz)
            shift = bias[jnp.minimum(o, 1)]
            score = mm_nt(key, qf[...]) * scale + jnp.concatenate([shift] * heads, axis=1)
            s_all[zz] = score
            dp_all[zz] = mm_nt(value, gf[...])
            old = m_row[...]
            new = jnp.maximum(old, jnp.max(score, axis=0, keepdims=True))
            weight = jnp.exp(score - new)
            fade = jnp.exp(old - new)
            m_row[...] = new
            l_row[...] = l_row[...] * fade + jnp.sum(weight, axis=0, keepdims=True)
            value_t = mm_nt(eye_low, value).astype(BF16)
            o_t[...] = o_t[...] * fade + mm(value_t, weight.astype(BF16))

        return carry

    lax.fori_loop(0, nz, forward, 0)

    attended_t = (o_t[...] * (1.0 / l_row[...])).astype(BF16)
    delta = jnp.sum(gt[...] * attended_t.astype(F32), axis=0, keepdims=True)
    log_total = m_row[...] + jnp.log(l_row[...])

    def send_x(i, value_t):
        for h in range(heads):
            x_out[i, :, pl.ds(h * dh, dh)] = mm_nt(eye_low, value_t[:, h * tok : (h + 1) * tok]).astype(BF16)
        along("x", x_out.at[i], r_out.at[i], xo_send.at[i], xo_recv.at[i])

    def send_y(i, dst):
        drain(others(r_out.at[i]), xo_recv.at[i])
        z_out[i] = mm(regroup, r_out[i]).astype(BF16)
        along("y", z_out.at[i], dst, yo_send.at[i], yo_recv.at[i])

    send_x(0, attended_t)

    def share(zz):
        drain(s_kv, part_recv.at[zz])
        comb[zz] = (part[zz, core].astype(F32) + sib_part[zz].astype(F32)).astype(BF16)
        remote(comb.at[zz], acc.at[z], acc_send.at[zz], acc_recv.at[z], at(y, x, zz)).start()

    def backward(i, carry):
        t = nz - 1 - i
        o = offset(t)
        last = offset(t + 2)

        @pl.when(z >= o)
        def _():
            zz = z - o
            key, value = pair(zz)
            prob = jnp.exp(s_all[zz] - log_total)
            score_grad = (prob * (dp_all[zz] - delta)).astype(BF16)
            key_t = mm_nt(eye_low, key).astype(BF16)
            value_part = mm(prob.astype(BF16), gf[...])
            key_part = mm(score_grad, qf[...]) * scale
            for b in range(2):
                part[zz, b, :, pl.ds(0, dh)] = key_part[b * tok : (b + 1) * tok].astype(BF16)
                part[zz, b, :, pl.ds(dh, dh)] = value_part[b * tok : (b + 1) * tok].astype(BF16)
            remote(part.at[zz, 1 - core], sib_part.at[zz], part_send.at[zz], part_recv.at[zz], sibling).start()
            dq_t[...] += mm(key_t, score_grad)

        @pl.when((t + 2 < nz) & (z >= last))
        def _():
            share(z - last)

        return carry

    lax.fori_loop(0, nz, backward, 0)

    @pl.when(z >= 1)
    def _():
        share(z - 1)

    send_x(1, (dq_t[...] * scale).astype(BF16))
    send_y(0, f_o)

    drain(s_kv, part_recv.at[z])
    total = part[z, core].astype(F32) + sib_part[z].astype(F32)
    for zz in range(nz):

        @pl.when(zz > z)
        def _():
            drain(s_kv, acc_recv.at[zz])

        @pl.when(zz <= z)
        def _():
            acc[zz] = jnp.zeros((tok, 2 * dh), BF16)

        total = total + acc[zz].astype(F32)
    s_dkv[...] = total.astype(BF16)
    along("x", s_dkv, r_dkv, xo_send.at[2], xo_recv.at[2])
    send_y(1, f_dq)
    drain(others(r_dkv), xo_recv.at[2])
    z_dkv[...] = mm(regroup, r_dkv[...]).astype(BF16)
    along("y", z_dkv, f_kv, yo_send.at[2], yo_recv.at[2])

    for i, (first_ref, second_ref) in enumerate(((in_kv, s_kv), (in_q, s_q), (s_g0, s_g))):
        drain(others(first_ref), a_send.at[i])
        drain(others(second_ref), b_send.at[i])
    for zz in range(nz):

        @pl.when(zz > z)
        def _():
            drain(s_kv, z_send.at[zz])

        @pl.when(zz < z)
        def _():
            drain(s_kv, acc_send.at[zz])

        @pl.when(zz <= z)
        def _():
            drain(s_kv, fwd_send.at[zz])
            drain(s_kv, part_send.at[zz])

    for i in range(2):
        drain(others(x_out.at[i]), xo_send.at[i])
        drain(others(z_out.at[i]), yo_send.at[i])
    drain(others(s_dkv), xo_send.at[2])
    drain(others(z_dkv), yo_send.at[2])
    drain(others(f_o), yo_recv.at[0])
    drain(others(f_dq), yo_recv.at[1])
    drain(others(f_kv), yo_recv.at[2])


def write_out(o_in, dq_in, kv_in, o_hbm, dq_hbm, dk_hbm, dv_hbm, sem):
    dh = dk_hbm.shape[1]
    copies = [
        pltpu.make_async_copy(o_in, o_hbm, sem.at[0]),
        pltpu.make_async_copy(dq_in, dq_hbm, sem.at[1]),
        pltpu.make_async_copy(kv_in.at[:, pl.ds(0, dh)], dk_hbm, sem.at[2]),
        pltpu.make_async_copy(kv_in.at[:, pl.ds(dh, dh)], dv_hbm, sem.at[3]),
    ]
    for copy in copies:
        copy.start()
    for copy in copies:
        copy.wait()


def local(ny, nx, nz, queries, keys, values, out_grad, doc_lengths, source_slot):
    tok, dh = keys.shape
    wide = queries.shape[1]
    heads = wide // dh
    flat = heads * tok
    docs = doc_lengths.shape[1]
    pad = -(-docs // 128) * 128
    dma = pltpu.SemaphoreType.DMA
    hbm = pl.BlockSpec(memory_space=pltpu.MemorySpace.HBM)
    vmem = pl.BlockSpec(memory_space=pltpu.VMEM)
    low = lambda *shape: pltpu.VMEM(shape, BF16)
    full = lambda *shape: pltpu.VMEM(shape, F32)
    whole = lambda *shape: pltpu.VMEM(shape, jnp.int32)
    found = pl.pallas_call(
        functools.partial(kernel, ny, nx, nz, heads),
        out_shape=(OUT(tok, wide), OUT(tok, wide), OUT(tok, 2 * dh)),
        in_specs=[hbm] * 6,
        out_specs=[vmem] * 3,
        scratch_shapes=[
            low(tok, 2 * dh), low(tok, wide), low(tok, wide), whole(1, docs), whole(1, tok),
            low(tok, 2 * dh), low(tok, wide), low(tok, wide),
            low(tok, 2 * dh), low(tok, wide), low(tok, wide), low(tok, wide),
            low(2 * nz, tok, 2 * dh), low(tok, wide), low(tok, wide),
            low(flat, dh), low(flat, dh), full(dh, flat),
            full(nz, 2 * tok, flat), full(nz, 2 * tok, flat),
            full(2, 2 * tok, tok), full(1, pad),
            full(1, flat), full(1, flat), full(dh, flat), full(dh, flat),
            low(2, tok, wide), low(2, tok, wide), low(2, tok, wide),
            low(nz, 2, tok, 2 * dh), low(nz, tok, 2 * dh), low(nz, tok, 2 * dh),
            low(nz, tok, 2 * dh), low(tok, 2 * dh), low(tok, 2 * dh), low(tok, 2 * dh),
            dma((6,)), dma((3,)), dma((3,)), dma((3,)), dma((3,)), dma((nz,)), dma((nz,)), dma((nz,)), dma((nz,)),
            dma((3,)), dma((3,)), dma((3,)), dma((3,)), dma((nz,)), dma((nz,)), dma((nz,)), dma((nz,)),
        ],
        compiler_params=pltpu.CompilerParams(collective_id=0, has_side_effects=True),
        name="packed_attention",
    )(queries, keys, values, out_grad, doc_lengths, source_slot.reshape(1, tok))
    shapes = [(tok, wide), (tok, wide), (tok, dh), (tok, dh)]
    return pl.pallas_call(
        write_out,
        out_shape=tuple(jax.ShapeDtypeStruct(shape, BF16) for shape in shapes),
        in_specs=[vmem] * 3,
        out_specs=[hbm] * 4,
        scratch_shapes=[dma((4,))],
        name="write_out",
    )(*[pltpu.with_memory_space_constraint(each, pltpu.VMEM) for each in found])


def solution(mesh):
    side = math.isqrt(mesh.shape["dp"])
    placed = (
        P(("dp", "ctx"), None),
        P(("dp", "ctx"), None),
        P(("dp", "ctx"), None),
        P(("dp", "ctx"), None),
        P("dp", None),
        P(("dp", "ctx")),
    )
    return jax.shard_map(
        functools.partial(local, side, side, mesh.shape["ctx"] // 2),
        mesh=mesh,
        in_specs=placed,
        out_specs=(
            P(("dp", "ctx"), None),
            P(("dp", "ctx"), None),
            P(("dp", "ctx"), None),
            P(("dp", "ctx"), None),
        ),
        check_vma=False,
    )
```

time: 75.5 us -> 72.2 us (0.956)
  local copies, waits for them, and re-layouts: 3.75 us -> 0 us
    unnamed x10 -> x0, local copies, waits for them, and re-layouts: 3.75 us -> none
    pallas_call x1 -> x2, Pallas kernels: 70.6 us -> 70.9 us  [the longest x1 70.2 us: local(): pl.pallas_call(functools.partial(kernel, ny, nx, nz, heads), out_shape=(O...]
where the time goes in v2:
time: 72.2 us; the launch traced here: 71.6 us
  Pallas kernels  70.9 us (98%)
    pallas_call x1, Pallas kernels, local(): pl.pallas_call(functools.partial(kernel, ny, nx, nz, heads), out_shape=(O...  70.2 us

profile of v2, /device:TPU:1, one launch (start us, length us, event | category | flops | bytes accessed | tf_op | source)
XLA Modules:
  0.0 71.6 jit_solution(17544003734980422813)
XLA Ops:
  0.6 70.2 %packed_attention.1 = (bf16[128,512]{1,0:T(8,128)(2,1)S(1)}, bf16[128,512]{1,0:T(8,128)(2,1)S(1)}, bf16[128,256]{1,0:T(8,128)(2,1)S(1)}) custom-call(bf16[128,512]{1,0:T(8,128)(2,1)} %q_hbm.1, bf16[128,128]{1,0:T(8,128)(2,1)} %k_hbm.1, bf16[128,128]{1,0:T(8,128)(2,1)} %v_hbm.1, bf16[128,512]{1,0:T(8,128)(2,1)} %g_hbm.1, s32[1,65]{1,0:T(1,128)} %lens_hbm.1, ...), custom_call_target="tpu_custom_call" | custom-call | tf_op jit(solution)/shard_map/packed_attention/pallas_call | solution.py:353
  70.8 0.7 %write_out.1 = (bf16[128,512]{1,0:T(8,128)(2,1)}, bf16[128,512]{1,0:T(8,128)(2,1)}, bf16[128,128]{1,0:T(8,128)(2,1)}, bf16[128,128]{1,0:T(8,128)(2,1)}) custom-call(bf16[128,512]{1,0:T(8,128)(2,1)S(1)} %get-tuple-element.7.o_in, bf16[128,512]{1,0:T(8,128)(2,1)S(1)} %get-tuple-element.8.dq_in, bf16[128,256]{1,0:T(8,128)(2,1)S(1)} %get-tuple-element.9.kv_in), custom_call_target="tpu_custom_call" | custom-call | tf_op jit(solution)/shard_map/write_out/pallas_call | solution.py:377

commit v3 on v2

--- a/solution.py
+++ b/solution.py
@@ -164,7 +164,7 @@
         remote(here, here, fwd_send.at[zz], fwd_recv.at[zz], sibling).start()
 
     def kv_out(i, carry):
-        o = offset(nz - 1 - i)
+        o = i + 1
 
         @pl.when(z + o < nz)
         def _():
@@ -189,8 +189,8 @@
         return both[:, :dh], both[:, dh:]
 
     def forward(t, carry):
-        o = offset(t)
-        nxt = offset(t + 1)
+        o = t
+        nxt = t + 1
 
         @pl.when((t + 1 < nz) & (z >= nxt))
         def _():

time: 72.2 us -> 70.4 us (0.975)
  Pallas kernels: 70.9 us -> 69.4 us
    pallas_call x1, Pallas kernels: 70.2 us -> 68.6 us  [local(): pl.pallas_call(functools.partial(kernel, ny, nx, nz, heads), out_shape=(O...]
where the time goes in v3:
time: 70.4 us; the launch traced here: 70 us
  Pallas kernels  69.4 us (99%)
    pallas_call x1, Pallas kernels, local(): pl.pallas_call(functools.partial(kernel, ny, nx, nz, heads), out_shape=(O...  68.6 us

profile of v3, /device:TPU:1, one launch (start us, length us, event | category | flops | bytes accessed | tf_op | source)
XLA Modules:
  0.0 70.0 jit_solution(7676863559769899282)
XLA Ops:
  0.6 68.6 %packed_attention.1 = (bf16[128,512]{1,0:T(8,128)(2,1)S(1)}, bf16[128,512]{1,0:T(8,128)(2,1)S(1)}, bf16[128,256]{1,0:T(8,128)(2,1)S(1)}) custom-call(bf16[128,512]{1,0:T(8,128)(2,1)} %q_hbm.1, bf16[128,128]{1,0:T(8,128)(2,1)} %k_hbm.1, bf16[128,128]{1,0:T(8,128)(2,1)} %v_hbm.1, bf16[128,512]{1,0:T(8,128)(2,1)} %g_hbm.1, s32[1,65]{1,0:T(1,128)} %lens_hbm.1, ...), custom_call_target="tpu_custom_call" | custom-call | tf_op jit(solution)/shard_map/packed_attention/pallas_call | solution.py:353
  69.2 0.7 %write_out.1 = (bf16[128,512]{1,0:T(8,128)(2,1)}, bf16[128,512]{1,0:T(8,128)(2,1)}, bf16[128,128]{1,0:T(8,128)(2,1)}, bf16[128,128]{1,0:T(8,128)(2,1)}) custom-call(bf16[128,512]{1,0:T(8,128)(2,1)S(1)} %get-tuple-element.7.o_in, bf16[128,512]{1,0:T(8,128)(2,1)S(1)} %get-tuple-element.8.dq_in, bf16[128,256]{1,0:T(8,128)(2,1)S(1)} %get-tuple-element.9.kv_in), custom_call_target="tpu_custom_call" | custom-call | tf_op jit(solution)/shard_map/write_out/pallas_call | solution.py:377

commit v4 on v3

--- a/solution.py
+++ b/solution.py
@@ -44,6 +44,7 @@
     x_out, r_out, z_out, part, sib_part, comb, acc, s_dkv, r_dkv, z_dkv,
     in_sem, a_send, a_recv, b_send, b_recv, z_send, z_recv, fwd_send, fwd_recv,
     xo_send, xo_recv, yo_send, yo_recv, part_send, part_recv, acc_send, acc_recv,
+    ready,
 ):
     tok = in_kv.shape[0]
     dh = k_hbm.shape[1]
@@ -88,9 +89,20 @@
         pl.semaphore_signal(barrier, inc=1, device_id=at((y + k) % ny, x, z), device_id_type=MESH)
     for k in far_first(nx):
         pl.semaphore_signal(barrier, inc=1, device_id=at(y, (x + k) % nx, z), device_id_type=MESH)
-    for k in far_first(nz):
-        pl.semaphore_signal(barrier, inc=1, device_id=at(y, x, (z + k) % nz), device_id_type=MESH)
     pl.semaphore_signal(barrier, inc=1, device_id=sibling, device_id_type=MESH)
+    late_line = (dp == 0) & (core == 0)
+    late = late_line & (z == 0)
+    for zz in range(1, nz):
+
+        @pl.when((zz > z) & jnp.logical_not(late))
+        def _():
+            pl.semaphore_signal(barrier, inc=1, device_id=at(y, x, zz), device_id_type=MESH)
+
+    @pl.when(late_line & (z > 0))
+    def _():
+        pl.semaphore_signal(barrier, inc=1, device_id=at(y, x, 0), device_id_type=MESH)
+
+    from_z = jnp.where(late, nz - 1, jnp.where(late_line, z - 1, z))
 
     loads = [
         pltpu.make_async_copy(g_hbm, in_g, in_sem.at[0]),
@@ -113,7 +125,13 @@
     s_g0[...] = mm(regroup, in_g[...]).astype(BF16)
     for load in loads[1:]:
         load.wait()
-    pl.semaphore_wait(barrier, ny + nx + nz - 2)
+    pl.semaphore_wait(barrier, ny + nx - 1 + from_z)
+    for zz in range(nz - 1):
+
+        @pl.when((zz < z) & jnp.logical_not(late_line & (zz == 0)))
+        def _():
+            pl.semaphore_signal(ready, inc=1, device_id=at(y, x, zz), device_id_type=MESH)
+
 
     along("y", in_kv, y_kv, a_send.at[0], a_recv.at[0])
     along("y", in_q, y_q, a_send.at[1], a_recv.at[1])
@@ -162,6 +180,10 @@
     def to_core(zz):
         here = kv_all.at[zz * 2 + core]
         remote(here, here, fwd_send.at[zz], fwd_recv.at[zz], sibling).start()
+
+    @pl.when(jnp.logical_not(late) & (z < nz - 1))
+    def _():
+        pl.semaphore_wait(ready, nz - 1 - z)
 
     def kv_out(i, carry):
         o = i + 1
@@ -369,6 +391,7 @@
             low(nz, tok, 2 * dh), low(tok, 2 * dh), low(tok, 2 * dh), low(tok, 2 * dh),
             dma((6,)), dma((3,)), dma((3,)), dma((3,)), dma((3,)), dma((nz,)), dma((nz,)), dma((nz,)), dma((nz,)),
             dma((3,)), dma((3,)), dma((3,)), dma((3,)), dma((nz,)), dma((nz,)), dma((nz,)), dma((nz,)),
+            pltpu.SemaphoreType.REGULAR,
         ],
         compiler_params=pltpu.CompilerParams(collective_id=0, has_side_effects=True),
         name="packed_attention",

time: 70.4 us -> 68.1 us (0.967)
  Pallas kernels: 69.4 us -> 67.3 us
    pallas_call x1, Pallas kernels: 68.6 us -> 66.6 us  [local(): pl.pallas_call(functools.partial(kernel, ny, nx, nz, heads), out_shape=(O...]
where the time goes in v4:
time: 68.1 us; the launch traced here: 68 us
  Pallas kernels  67.3 us (99%)
    pallas_call x1, Pallas kernels, local(): pl.pallas_call(functools.partial(kernel, ny, nx, nz, heads), out_shape=(O...  66.6 us

profile of v4, /device:TPU:1, one launch (start us, length us, event | category | flops | bytes accessed | tf_op | source)
XLA Modules:
  0.0 68.0 jit_solution(9458830184409034102)
XLA Ops:
  0.6 66.6 %packed_attention.1 = (bf16[128,512]{1,0:T(8,128)(2,1)S(1)}, bf16[128,512]{1,0:T(8,128)(2,1)S(1)}, bf16[128,256]{1,0:T(8,128)(2,1)S(1)}) custom-call(bf16[128,512]{1,0:T(8,128)(2,1)} %q_hbm.1, bf16[128,128]{1,0:T(8,128)(2,1)} %k_hbm.1, bf16[128,128]{1,0:T(8,128)(2,1)} %v_hbm.1, bf16[128,512]{1,0:T(8,128)(2,1)} %g_hbm.1, s32[1,65]{1,0:T(1,128)} %lens_hbm.1, ...), custom_call_target="tpu_custom_call" | custom-call | tf_op jit(solution)/shard_map/packed_attention/pallas_call | solution.py:375
  67.2 0.7 %write_out.1 = (bf16[128,512]{1,0:T(8,128)(2,1)}, bf16[128,512]{1,0:T(8,128)(2,1)}, bf16[128,128]{1,0:T(8,128)(2,1)}, bf16[128,128]{1,0:T(8,128)(2,1)}) custom-call(bf16[128,512]{1,0:T(8,128)(2,1)S(1)} %get-tuple-element.7.o_in, bf16[128,512]{1,0:T(8,128)(2,1)S(1)} %get-tuple-element.8.dq_in, bf16[128,256]{1,0:T(8,128)(2,1)S(1)} %get-tuple-element.9.kv_in), custom_call_target="tpu_custom_call" | custom-call | tf_op jit(solution)/shard_map/write_out/pallas_call | solution.py:400

commit v5 on v4

--- a/solution.py
+++ b/solution.py
@@ -210,11 +210,21 @@
         both = kv_all[pl.ds(zz * 2, 2)].reshape(2 * tok, 2 * dh)
         return both[:, :dh], both[:, dh:]
 
+    def hop(t):
+        return jnp.where((t == 0) | (t >= z), t, z - t)
+
+    second = jnp.where(z <= 1, 1, z - 1)
+
+    @pl.when(z >= second)
+    def _():
+        drain(s_kv, z_recv.at[z - second])
+        to_core(z - second)
+
     def forward(t, carry):
-        o = t
-        nxt = t + 1
-
-        @pl.when((t + 1 < nz) & (z >= nxt))
+        o = hop(t)
+        nxt = hop(t + 2)
+
+        @pl.when((t + 2 < nz) & (z >= nxt))
         def _():
             drain(s_kv, z_recv.at[z - nxt])
             to_core(z - nxt)
@@ -265,7 +275,7 @@
     def backward(i, carry):
         t = nz - 1 - i
         o = offset(t)
-        last = offset(t + 2)
+        last = offset(t + 3)
 
         @pl.when(z >= o)
         def _():
@@ -282,13 +292,19 @@
             remote(part.at[zz, 1 - core], sib_part.at[zz], part_send.at[zz], part_recv.at[zz], sibling).start()
             dq_t[...] += mm(key_t, score_grad)
 
-        @pl.when((t + 2 < nz) & (z >= last))
+        @pl.when((t + 3 < nz) & (z >= last))
         def _():
             share(z - last)
 
         return carry
 
     lax.fori_loop(0, nz, backward, 0)
+
+    if nz > 2:
+
+        @pl.when(z >= nz - 1)
+        def _():
+            share(z - (nz - 1))
 
     @pl.when(z >= 1)
     def _():

time: 68.1 us -> 67 us (0.984)
  Pallas kernels: 67.3 us -> 65.9 us
    pallas_call x1, Pallas kernels: 66.6 us -> 65.2 us  [local(): pl.pallas_call(functools.partial(kernel, ny, nx, nz, heads), out_shape=(O...]
where the time goes in v5:
time: 67 us; the launch traced here: 66.5 us
  Pallas kernels  65.9 us (98%)
    pallas_call x1, Pallas kernels, local(): pl.pallas_call(functools.partial(kernel, ny, nx, nz, heads), out_shape=(O...  65.2 us

profile of v5, /device:TPU:1, one launch (start us, length us, event | category | flops | bytes accessed | tf_op | source)
XLA Modules:
  0.0 66.5 jit_solution(2111459339740214240)
XLA Ops:
  0.6 65.2 %packed_attention.1 = (bf16[128,512]{1,0:T(8,128)(2,1)S(1)}, bf16[128,512]{1,0:T(8,128)(2,1)S(1)}, bf16[128,256]{1,0:T(8,128)(2,1)S(1)}) custom-call(bf16[128,512]{1,0:T(8,128)(2,1)} %q_hbm.1, bf16[128,128]{1,0:T(8,128)(2,1)} %k_hbm.1, bf16[128,128]{1,0:T(8,128)(2,1)} %v_hbm.1, bf16[128,512]{1,0:T(8,128)(2,1)} %g_hbm.1, s32[1,65]{1,0:T(1,128)} %lens_hbm.1, ...), custom_call_target="tpu_custom_call" | custom-call | tf_op jit(solution)/shard_map/packed_attention/pallas_call | solution.py:391
  65.8 0.7 %write_out.1 = (bf16[128,512]{1,0:T(8,128)(2,1)}, bf16[128,512]{1,0:T(8,128)(2,1)}, bf16[128,128]{1,0:T(8,128)(2,1)}, bf16[128,128]{1,0:T(8,128)(2,1)}) custom-call(bf16[128,512]{1,0:T(8,128)(2,1)S(1)} %get-tuple-element.7.o_in, bf16[128,512]{1,0:T(8,128)(2,1)S(1)} %get-tuple-element.8.dq_in, bf16[128,256]{1,0:T(8,128)(2,1)S(1)} %get-tuple-element.9.kv_in), custom_call_target="tpu_custom_call" | custom-call | tf_op jit(solution)/shard_map/write_out/pallas_call | solution.py:416

commit v6 on v5

--- a/solution.py
+++ b/solution.py
@@ -121,8 +121,6 @@
     eye = (row_i == col_i).astype(F32)
     eye_low = eye.astype(BF16)
 
-    loads[0].wait()
-    s_g0[...] = mm(regroup, in_g[...]).astype(BF16)
     for load in loads[1:]:
         load.wait()
     pl.semaphore_wait(barrier, ny + nx - 1 + from_z)
@@ -130,11 +128,13 @@
 
         @pl.when((zz < z) & jnp.logical_not(late_line & (zz == 0)))
         def _():
-            pl.semaphore_signal(ready, inc=1, device_id=at(y, x, zz), device_id_type=MESH)
+            pl.semaphore_signal(ready.at[z], inc=1, device_id=at(y, x, zz), device_id_type=MESH)
 
 
     along("y", in_kv, y_kv, a_send.at[0], a_recv.at[0])
     along("y", in_q, y_q, a_send.at[1], a_recv.at[1])
+    loads[0].wait()
+    s_g0[...] = mm(regroup, in_g[...]).astype(BF16)
     along("x", s_g0, x_g, a_send.at[2], a_recv.at[2])
 
     slot = slot_in[...]
@@ -181,12 +181,12 @@
         here = kv_all.at[zz * 2 + core]
         remote(here, here, fwd_send.at[zz], fwd_recv.at[zz], sibling).start()
 
-    @pl.when(jnp.logical_not(late) & (z < nz - 1))
-    def _():
-        pl.semaphore_wait(ready, nz - 1 - z)
-
     def kv_out(i, carry):
         o = i + 1
+
+        @pl.when((z + o < nz) & jnp.logical_not(late))
+        def _():
+            pl.semaphore_wait(ready.at[z + o], 1)
 
         @pl.when(z + o < nz)
         def _():
@@ -407,7 +407,7 @@
             low(nz, tok, 2 * dh), low(tok, 2 * dh), low(tok, 2 * dh), low(tok, 2 * dh),
             dma((6,)), dma((3,)), dma((3,)), dma((3,)), dma((3,)), dma((nz,)), dma((nz,)), dma((nz,)), dma((nz,)),
             dma((3,)), dma((3,)), dma((3,)), dma((3,)), dma((nz,)), dma((nz,)), dma((nz,)), dma((nz,)),
-            pltpu.SemaphoreType.REGULAR,
+            pltpu.SemaphoreType.REGULAR((nz,)),
         ],
         compiler_params=pltpu.CompilerParams(collective_id=0, has_side_effects=True),
         name="packed_attention",

time: 67 us -> 65.1 us (0.972)
  Pallas kernels: 65.9 us -> 64.3 us
    pallas_call x1, Pallas kernels: 65.2 us -> 63.5 us  [local(): pl.pallas_call(functools.partial(kernel, ny, nx, nz, heads), out_shape=(O...]
where the time goes in v6:
time: 65.1 us; the launch traced here: 64.9 us
  Pallas kernels  64.3 us (99%)
    pallas_call x1, Pallas kernels, local(): pl.pallas_call(functools.partial(kernel, ny, nx, nz, heads), out_shape=(O...  63.5 us

profile of v6, /device:TPU:1, one launch (start us, length us, event | category | flops | bytes accessed | tf_op | source)
XLA Modules:
  0.0 64.9 jit_solution(5220848542566466591)
XLA Ops:
  0.6 63.5 %packed_attention.1 = (bf16[128,512]{1,0:T(8,128)(2,1)S(1)}, bf16[128,512]{1,0:T(8,128)(2,1)S(1)}, bf16[128,256]{1,0:T(8,128)(2,1)S(1)}) custom-call(bf16[128,512]{1,0:T(8,128)(2,1)} %q_hbm.1, bf16[128,128]{1,0:T(8,128)(2,1)} %k_hbm.1, bf16[128,128]{1,0:T(8,128)(2,1)} %v_hbm.1, bf16[128,512]{1,0:T(8,128)(2,1)} %g_hbm.1, s32[1,65]{1,0:T(1,128)} %lens_hbm.1, ...), custom_call_target="tpu_custom_call" | custom-call | tf_op jit(solution)/shard_map/packed_attention/pallas_call | solution.py:391
  64.2 0.7 %write_out.1 = (bf16[128,512]{1,0:T(8,128)(2,1)}, bf16[128,512]{1,0:T(8,128)(2,1)}, bf16[128,128]{1,0:T(8,128)(2,1)}, bf16[128,128]{1,0:T(8,128)(2,1)}) custom-call(bf16[128,512]{1,0:T(8,128)(2,1)S(1)} %get-tuple-element.7.o_in, bf16[128,512]{1,0:T(8,128)(2,1)S(1)} %get-tuple-element.8.dq_in, bf16[128,256]{1,0:T(8,128)(2,1)S(1)} %get-tuple-element.9.kv_in), custom_call_target="tpu_custom_call" | custom-call | tf_op jit(solution)/shard_map/write_out/pallas_call | solution.py:416
